TPU v7x, 32 devices: a whole 2x2x4 slice. The times are simulated.
32 devices in a mesh: tok: 2 (over core), head: 4 (over y, x), exp: 4 (over z).
Axes of the slice: x: 2, y: 2, z: 4, core: 2. Of those that a mesh axis runs over, the one named last changes fastest.
Arguments:
- context: bfloat16 [4, 64, 4096], P('exp', 'tok', 'head'), may hold values from -6 to 6
- out_proj: bfloat16 [4096, 4096], P('head', 'exp'), may hold values from -0.125 to 0.125
- stream: float32 [4, 64, 4096], P('exp', 'tok', 'head'), may hold values from -75 to 75
- norm_gain: float32 [4096], replicated, may hold values from 0.1 to 1.9
- expert_ids: int32 [4, 64, 8], P('exp', 'tok'), may hold values from 0 to 31, as said below
- slot_ids: int32 [4, 64, 8], P('exp', 'tok'), may hold values from -1 to 11, as said below
- gate_probs: float32 [4, 64, 8], P('exp', 'tok'), may hold values from 0.02 to 0.3
- w_gate: bfloat16 [32, 3072, 4096], P(('tok', 'exp'), 'head'), may hold values from -0.09375 to 0.09375
- w_up: bfloat16 [32, 3072, 4096], P(('tok', 'exp'), 'head'), may hold values from -0.09375 to 0.09375
- w_down: bfloat16 [32, 3072, 4096], P(('tok', 'exp'), 'head'), may hold values from -0.15625 to 0.15625
Outputs:
- mixed: float32 [4, 64, 4096], P('exp', 'tok', 'head')
Inputs may be any that keep to these rules, and one draw needn't show every extreme that they name: `expert_ids`: each token names 8 different experts. `slot_ids`: within a block of 32 consecutive tokens of one image, the choices of one expert take slots 0, 1, 2, ... in token order until its 12 slots are full, later ones get -1; in every block some expert fills all 12 slots.
All inputs are finite; a program needn't handle non-finite values.
Results may differ from a plain program's by a relative error of at most 0.0034.
Values may be sent and summed in bfloat16 or wider, within the bound.
A program may use at most 128 MiB of HBM per device.

v0:
```python
import jax
import jax.numpy as jnp
from jax import lax
from jax.sharding import PartitionSpec as P

EXPERTS = 32
TOP = 8
CAP = 12


eps_value = 1e-05


def on_device(
    context, out_proj, stream, norm_gain, expert_ids, slot_ids, gate_probs, w_gate, w_up, w_down
):
    local_context = context[0]
    own_stream = stream[0]
    col_width = own_stream.shape[1]
    col_start = lax.axis_index("head") * col_width
    partial_value = jnp.dot(
        local_context,
        lax.all_gather(out_proj, "exp", axis=1, tiled=True),
        preferred_element_type=jnp.float32,
    )
    own_sum = lax.dynamic_slice_in_dim(partial_value, col_start, col_width, 1) + own_stream
    partial_value = lax.dynamic_update_slice_in_dim(partial_value, own_sum, col_start, 1)
    resid_full = lax.psum(partial_value, "head")
    resid_own = lax.dynamic_slice_in_dim(resid_full, col_start, col_width, 1)
    mean_sq = jnp.mean(resid_full * resid_full, axis=1, keepdims=True)
    gain_own = lax.dynamic_slice_in_dim(norm_gain, col_start, col_width, 0)
    normed_own = (resid_own * lax.rsqrt(mean_sq + eps_value) * gain_own).astype(jnp.bfloat16)
    choice_ids = expert_ids[0]
    choice_slots = slot_ids[0]
    weights = gate_probs[0]
    spill_slot = EXPERTS * CAP
    target = jnp.where(choice_slots >= 0, choice_ids * CAP + choice_slots, spill_slot)
    outgoing = (
        jnp.zeros((spill_slot + 1, col_width), jnp.bfloat16)
        .at[target.reshape(-1)]
        .set(jnp.repeat(normed_own, TOP, axis=0))
    )
    outgoing = outgoing[:spill_slot].reshape(EXPERTS, CAP, col_width)
    tok_count = lax.axis_size("tok")
    groups = tok_count * lax.axis_size("exp")
    local_experts = w_gate.shape[0]
    arrived = lax.all_to_all(outgoing, ("tok", "exp"), split_axis=0, concat_axis=0, tiled=True)
    arrived = arrived.reshape(groups, local_experts, CAP, col_width)
    piece = lax.all_gather(arrived, "head", axis=3, tiled=True)
    gate_more = jnp.einsum("slcd,lhd->slch", piece, w_gate, preferred_element_type=jnp.float32)
    up_more = jnp.einsum("slcd,lhd->slch", piece, w_up, preferred_element_type=jnp.float32)
    hidden = (jax.nn.silu(gate_more) * up_more).astype(jnp.bfloat16)
    produced = jnp.einsum(
        "slch,lhd->slcd", hidden, w_down, preferred_element_type=jnp.float32
    ).astype(jnp.bfloat16)
    widened = lax.optimization_barrier(produced).astype(jnp.float32)
    summed = lax.psum_scatter(
        widened.astype(jnp.bfloat16), "head", scatter_dimension=3, tiled=True
    ).astype(jnp.float32)
    returned_share = lax.all_to_all(
        summed.reshape(EXPERTS, CAP, col_width).astype(jnp.bfloat16),
        ("tok", "exp"),
        split_axis=0,
        concat_axis=0,
        tiled=True,
    ).astype(jnp.float32)
    lookup_share = jnp.concatenate(
        [returned_share.reshape(spill_slot, col_width), jnp.zeros((1, col_width), jnp.float32)],
        axis=0,
    )
    picked_share = lookup_share[target]
    expert_own = jnp.sum(picked_share * weights[:, :, None], axis=1)
    return (resid_own + expert_own)[None]


def solution(mesh):
    in_specs = (
        P("exp", "tok", "head"),
        P("head", "exp"),
        P("exp", "tok", "head"),
        P(),
        P("exp", "tok", None),
        P("exp", "tok", None),
        P("exp", "tok", None),
        P(("tok", "exp"), "head", None),
        P(("tok", "exp"), "head", None),
        P(("tok", "exp"), "head", None),
    )
    out_specs = P("exp", "tok", "head")
    return jax.shard_map(
        on_device, mesh=mesh, in_specs=in_specs, out_specs=out_specs, check_vma=False
    )
```

profile of v0, /device:TPU:15, one launch (start us, length us, event | category | flops | bytes accessed | tf_op | source)
XLA Modules:
  0.0 428.4 jit_solution(15233698592753137792)
XLA Ops:
  6.5 0.0 copy-start
  6.5 0.0 all-gather.3.cloned.1.call-start
  6.5 0.7 all-gather.3.cloned.1.call-update
  7.3 0.0 all-reduce.3.cloned.1.call-start
  7.3 0.0 copy-start.3
  7.3 0.0 copy-start.5
  7.3 0.0 copy-start.6
  7.3 0.0 dynamic-slice-start
  7.4 149.4 %all-gather.3.cloned.1.call-done = bf16[1024,4096]{1,0:T(8,128)(2,1)} async-done(((bf16[1024,1024]{1,0:T(8,128)(2,1)}), bf16[1024,4096]{1,0:T(8,128)(2,1)}) %all-gather.3.cloned.1.call-update) | async-done | bytes 8388624 | tf_op jit(solution)/shard_map/all_gather | solution.py:23
  156.7 0.0 copy-done
  156.7 4.9 %fusion.24 = f32[32,4096]{1,0:T(8,128)S(1)} fusion(bf16[1024,4096]{1,0:T(8,128)(2,1)} %all-gather.3.cloned.1.call-done, bf16[1,32,1024]{2,1,0:T(8,128)(2,1)S(1)} %copy-done), kind=kOutput, calls=%fused_computation.29 | convolution fusion | flops 268435456 | bytes 8978432 | tf_op jit(solution)/shard_map/dot_general | solution.py:21
  161.6 0.0 copy-done.3
  161.7 0.0 copy-start.2
  161.7 0.8 copy-done.2
  162.5 0.0 all-reduce.3.cloned.1.call-update
  162.5 0.0 all-gather.5.cloned.1.call-start
  162.6 0.0 copy-done.5
  162.6 0.0 copy-done.6
  162.6 0.1 copy.19
  162.7 0.1 select_n.53
  162.8 44.9 %all-reduce.3.cloned.1.call-done = f32[32,4096]{1,0:T(8,128)} async-done(((f32[32,4096]{1,0:T(8,128)}), f32[32,4096]{1,0:T(8,128)}) %all-reduce.3.cloned.1.call-update) | async-done | bytes 524304 | tf_op jit(solution)/shard_map/psum | solution.py:28
  207.7 1.2 multiply_reduce_fusion
  208.9 1.0 multiply_convert_fusion
  209.9 1.9 scatter_custom_fusion
  211.8 0.1 slice.6
  211.9 0.2 reshape.125
  212.0 29.7 %all_to_all.10 = bf16[32,12,1024]{2,1,0:T(8,128)(2,1)S(1)} all-to-all(bf16[32,12,1024]{2,1,0:T(8,128)(2,1)S(1)} %reshape.125), channel_id=1, replica_groups=mesh['tok'=2,'head'=4,'exp'=4] {'tok','exp'}, dimensions={0} | all-to-all | bytes 1572864 | tf_op jit(solution)/shard_map/all_to_all | solution.py:47
  241.8 1.0 copy.21
  242.8 0.0 all-gather.5.cloned.1.call-update
  242.8 0.2 reduce-scatter.2.cloned.1.call-start
  243.0 51.2 %all-gather.5.cloned.1.call-done = bf16[8,4,12,4096]{3,2,0,1:T(8,128)(2,1)} async-done(((bf16[8,4,12,1024]{3,2,0,1:T(8,128)(2,1)}), bf16[8,4,12,4096]{3,2,0,1:T(8,128)(2,1)}) %all-gather.5.cloned.1.call-update) | async-done | bytes 3145744 | tf_op jit(solution)/shard_map/all_gather | solution.py:49
  294.3 13.4 %fusion.4 = f32[4,8,12,768]{3,2,1,0:T(8,128)S(1)} fusion(bf16[8,4,12,4096]{3,2,0,1:T(8,128)(2,1)} %all-gather.5.cloned.1.call-done, bf16[4,768,4096]{2,1,0:T(8,128)(2,1)} %param.17), kind=kOutput, calls=%fused_computation.6 | convolution fusion | flops 2415919104 | bytes 29491200 | tf_op jit(solution)/shard_map/slcd,lhd->slch/dot_general | solution.py:50
  307.7 13.5 %fusion.12 = bf16[8,4,12,768]{3,2,0,1:T(8,128)(2,1)S(1)} fusion(f32[4,8,12,768]{3,2,1,0:T(8,128)S(1)} %fusion.4, bf16[8,4,12,4096]{3,2,0,1:T(8,128)(2,1)} %all-gather.5.cloned.1.call-done, bf16[4,768,4096]{2,1,0:T(8,128)(2,1)} %param.18), kind=kOutput, calls=%fused_computation.11 | convolution fusion | flops 2417688576 | bytes 30081024 | tf_op jit(solution)/shard_map/slcd,lhd->slch/dot_general | solution.py:51
  321.2 13.6 %fusion.9 = bf16[8,4,12,4096]{3,2,0,1:T(8,128)(2,1)} fusion(bf16[8,4,12,768]{3,2,0,1:T(8,128)(2,1)S(1)} %fusion.12, bf16[4,768,4096]{2,1,0:T(8,128)(2,1)} %param.19), kind=kOutput, calls=%fused_computation.9 | convolution fusion | flops 2417491968 | bytes 28901376 | tf_op jit(solution)/shard_map/slch,lhd->slcd/dot_general | solution.py:53
  334.7 0.0 reduce-scatter.2.cloned.1.call-update
  334.8 52.7 %reduce-scatter.2.cloned.1.call-done = bf16[8,4,12,1024]{3,2,0,1:T(8,128)(2,1)} async-done(((bf16[8,4,12,4096]{3,2,0,1:T(8,128)(2,1)}), bf16[8,4,12,1024]{3,2,0,1:T(8,128)(2,1)}) %reduce-scatter.2.cloned.1.call-update) | async-done | bytes 786448 | tf_op jit(solution)/shard_map/reduce_scatter | solution.py:57
  387.5 2.3 copy.31
  389.8 5.6 %all-to-all-start.1 = ((bf16[32,12,1024]{2,1,0:T(8,128)(2,1)}), bf16[32,12,1024]{2,1,0:T(8,128)(2,1)S(1)}, u32[]{:S(2)}, u32[]{:S(2)}) async-start(bf16[32,12,1024]{2,1,0:T(8,128)(2,1)} %bitcast.14), calls=%async_computation.2 | async-start | bytes 2097152 | tf_op jit(solution)/shard_map/all_to_all | solution.py:60
  395.4 0.1 copy.24
  395.5 0.1 reshape.130
  395.6 0.1 copy.25
  395.7 22.9 %all-to-all-done.1 = bf16[32,12,1024]{2,1,0:T(8,128)(2,1)S(1)} async-done(((bf16[32,12,1024]{2,1,0:T(8,128)(2,1)}), bf16[32,12,1024]{2,1,0:T(8,128)(2,1)S(1)}, u32[]{:S(2)}, u32[]{:S(2)}) %all-to-all-start.1) | async-done | bytes 786464 | tf_op jit(solution)/shard_map/all_to_all | solution.py:60
  418.5 0.2 reshape.127
  418.7 0.0 copy-start.1
  418.7 0.2 pad_convert_fusion
  418.9 1.1 gather_fusion
  420.0 0.4 fusion.18
  420.3 1.6 add_bitcast_fusion
  (9 shorter events, 0.1 us)
Async XLA Ops:
  6.5 150.2 %copy-start = (bf16[1,32,1024]{2,1,0:T(8,128)(2,1)S(1)}, bf16[1,32,1024]{2,1,0:T(8,128)(2,1)}, u32[]{:S(2)}) copy-start(bf16[1,32,1024]{2,1,0:T(8,128)(2,1)} %param.10) | copy-start | bytes 196612
  6.5 150.2 %all-gather.3.cloned.1.call-start = ((), (), s32[]{:S(2)}) async-start(), calls=%async_computation.3 | async-start | bytes 10485760 | tf_op jit(solution)/shard_map/all_gather | solution.py:23
  7.3 200.4 %all-reduce.3.cloned.1.call-start = ((), (), s32[]{:S(2)}) async-start(), calls=%async_computation.4 | async-start | bytes 1048576 | tf_op jit(solution)/shard_map/psum | solution.py:28
  7.3 154.3 %copy-start.3 = (f32[1,32,1024]{2,1,0:T(8,128)S(1)}, f32[1,32,1024]{2,1,0:T(8,128)}, u32[]{:S(2)}) copy-start(f32[1,32,1024]{2,1,0:T(8,128)} %param.12) | copy-start | bytes 393220
  7.3 155.2 %copy-start.5 = (s32[1,32,8]{1,2,0:T(8,128)S(1)}, s32[1,32,8]{1,2,0:T(8,128)}, u32[]{:S(2)}) copy-start(s32[1,32,8]{1,2,0:T(8,128)} %param.15) | copy-start | bytes 3076
  7.3 155.2 %copy-start.6 = (s32[1,32,8]{1,2,0:T(8,128)S(1)}, s32[1,32,8]{1,2,0:T(8,128)}, u32[]{:S(2)}) copy-start(s32[1,32,8]{1,2,0:T(8,128)} %param.14) | copy-start | bytes 3076
  7.3 201.6 %dynamic-slice-start = ((f32[4096]{0:T(1024)}, s32[]{:T(128)}), f32[1024]{0:T(1024)S(1)}, s32[]{:S(2)}) async-start(f32[4096]{0:T(1024)} %param.13, s32[]{:T(128)} %select_n.51), calls=%async_computation.7 | async-start | bytes 8704 | tf_op jit(solution)/shard_map/dynamic_slice | solution.py:31
  161.7 0.8 copy-start.2
  162.5 131.7 %all-gather.5.cloned.1.call-start = ((), (), s32[]{:S(2)}) async-start(), calls=%async_computation.5 | async-start | bytes 5242880 | tf_op jit(solution)/shard_map/all_gather | solution.py:49
  242.8 144.7 %reduce-scatter.2.cloned.1.call-start = ((), (), s32[]{:S(2)}) async-start(), calls=%async_computation.6 | async-start | bytes 5242880 | tf_op jit(solution)/shard_map/reduce_scatter | solution.py:57
  334.7 60.8 %copy-start.4 = (f32[1,32,8]{1,2,0:T(8,128)S(1)}, f32[1,32,8]{1,2,0:T(8,128)}, u32[]{:S(2)}) copy-start(f32[1,32,8]{1,2,0:T(8,128)} %param.16) | copy-start | bytes 3076
  389.8 28.7 %all-to-all-start.1 = ((bf16[32,12,1024]{2,1,0:T(8,128)(2,1)}), bf16[32,12,1024]{2,1,0:T(8,128)(2,1)S(1)}, u32[]{:S(2)}, u32[]{:S(2)}) async-start(bf16[32,12,1024]{2,1,0:T(8,128)(2,1)} %bitcast.14), calls=%async_computation.2 | async-start | bytes 2097152 | tf_op jit(solution)/shard_map/all_to_all | solution.py:60
  418.7 3.2 copy-start.1
Sparse Core Ops, SparseCore 0:
  8.9 147.7 all-gather.2
  162.6 45.0 all-reduce.2
  242.9 51.2 all-gather.4
  334.9 52.5 reduce-scatter.1
where the time goes:
time: 433 us; the launch traced here: 428 us
  waiting for transfers between devices  322 us (74%)
  matrix products  45.4 us (10%)
  blocking collectives  29.7 us (7%)
  between operations  13.3 us (3%)
  local copies, waits for them, and re-layouts  7.94 us (2%)
  starting transfers between devices  5.89 us (1%)
  other arithmetic  4.33 us (1%)
    all_gather x1, waiting for transfers between devices, on_device(): lax.all_gather(out_proj, 'exp', axis=1, tiled=True)  149 us
    reduce_scatter x1, waiting for transfers between devices, on_device(): lax.psum_scatter(widened.astype(jnp.bfloat16), 'head', scatter_dimension=...  52.7 us
    all_gather x1, waiting for transfers between devices, on_device(): piece = lax.all_gather(arrived, 'head', axis=3, tiled=True)  51.2 us
    psum x1, waiting for transfers between devices, on_device(): resid_full = lax.psum(partial_value, 'head')  44.9 us
    all_to_all x1, blocking collectives, on_device(): lax.all_to_all(outgoing, ('tok', 'exp'), split_axis=0, concat_axis=0, til...  29.7 us
    all_to_all x1, waiting for transfers between devices, on_device(): lax.all_to_all(summed.reshape(EXPERTS, CAP, col_width).astype(jnp.bfloat1...  22.9 us
    dot_general x1, matrix products, on_device(): jnp.einsum('slch,lhd->slcd', hidden, w_down, preferred_element_type=jnp.f...  13.6 us
    dot_general x1, matrix products, on_device(): jnp.einsum('slcd,lhd->slch', piece, w_up, preferred_element_type=jnp.floa...  13.5 us
  transfers between devices with their start and end apart: 5, of which 5 were waited for; matrix products, arithmetic and copies ran while one was open for 0% of the time, Pallas kernels for 0%

commit v1 on v0

v1 whole, which is shorter than its diff:
```python
import functools

import jax
import jax.numpy as jnp
from jax import lax
from jax.experimental import pallas as pl
from jax.experimental.pallas import tpu as pltpu
from jax.sharding import PartitionSpec as P

MESH = pl.DeviceIdType.MESH
LANES = 128
SLOT_BYTES = 50_400_000
F32 = jnp.float32
BF16 = jnp.bfloat16
eps_value = 1e-05


def kernel(
    n_tok, n_head, n_exp, n_slots,
    ctx_ref, proj_hbm, stream_ref, gain_ref, ids_ref, slots_ref, probs_ref,
    wg_hbm, wu_hbm, wd_hbm,
    out_ref,
    proj, wbuf, ctx_all, wall, stream_bf, stream_t, pbf, pown, prs,
    attn_buf, attn_in, ssq, x, hid, acc, obf, tin, hsend, hrecv, zsend, zrecv,
    proj_sem, w_sem, ctx_s, ctx_r, wz_s, wz_r, wt_s, wt_r, st_s, st_r,
    prs_s, prs_r, at_s, at_r, xz_s, xz_r, qz_s, qz_r, xh_s, xh_r, qh_s, qh_r,
    xt_s, xt_r, qt_s, qt_r, to_s, to_r, ho_s, ho_r, zo_s, zo_r,
):
    t, h, e = lax.axis_index("tok"), lax.axis_index("head"), lax.axis_index("exp")
    rows, width = stream_ref.shape
    n_local, n_hid, model = wg_hbm.shape
    tokens = n_tok * n_exp * rows
    tp = 1 - t
    turned = {"tok": t, "head": e, "exp": h}
    mine = h == e

    def send(src, dst, s_sem, r_sem, device):
        return pltpu.make_async_remote_copy(
            src_ref=src, dst_ref=dst, send_sem=s_sem, recv_sem=r_sem,
            device_id=device, device_id_type=MESH,
        )

    def on_exp(k):
        return {"exp": lax.rem(e + k, n_exp)}

    def on_head(k):
        return {"head": lax.rem(h + k, n_head)}

    on_tok = {"tok": tp}

    sources = (wg_hbm, wu_hbm, wd_hbm)

    def w_copy(q):
        return pltpu.make_async_copy(
            sources[q % 3].at[q // 3], wbuf.at[q % n_slots], w_sem.at[q % n_slots]
        )

    proj_copy = pltpu.make_async_copy(proj_hbm, proj, proj_sem)
    proj_copy.start()

    barrier = pltpu.get_barrier_semaphore()
    for k in range(1, n_exp):
        pl.semaphore_signal(barrier, inc=1, device_id=on_exp(k), device_id_type=MESH)
    for k in range(1, n_head):
        pl.semaphore_signal(barrier, inc=1, device_id=on_head(k), device_id_type=MESH)
    pl.semaphore_signal(barrier, inc=1, device_id=on_tok, device_id_type=MESH)

    @pl.when(jnp.logical_not(mine))
    def _():
        pl.semaphore_signal(barrier, inc=1, device_id=turned, device_id_type=MESH)

    for q in range(n_slots):
        w_copy(q).start()
    stream_bf[...] = stream_ref[...].astype(BF16)
    lane = lax.broadcasted_iota(jnp.int32, (rows, LANES), 1)
    dense = jnp.zeros((rows, LANES), F32)
    for k in range(ids_ref.shape[1]):
        hit = (ids_ref[:, k : k + 1] == lane) & (slots_ref[:, k : k + 1] >= 0)
        dense = dense + jnp.where(hit, probs_ref[:, k : k + 1], 0.0)
    wall[t, e] = dense
    ctx_all[e] = ctx_ref[...]

    @pl.when(mine)
    def _():
        pl.semaphore_wait(barrier, n_exp - 1 + n_head - 1 + 1)

    @pl.when(jnp.logical_not(mine))
    def _():
        pl.semaphore_wait(barrier, n_exp - 1 + n_head - 1 + 2)

    ctx_c = [
        send(ctx_ref, ctx_all.at[e], ctx_s.at[k], ctx_r.at[k], on_exp(k)) for k in range(1, n_exp)
    ]
    for c in ctx_c:
        c.start()
    stream_c = send(stream_bf, stream_t, st_s, st_r, turned)

    @pl.when(jnp.logical_not(mine))
    def _():
        stream_c.start()

    wz_c = [
        send(wall.at[t, e], wall.at[t, e], wz_s.at[k], wz_r.at[k], on_exp(k))
        for k in range(1, n_exp)
    ]
    for c in wz_c:
        c.start()
    proj_copy.wait()
    for c in ctx_c:
        c.wait()

    tile = min(width, 256)

    def project(i, carry):
        cols = pl.ds(pl.multiple_of(i * tile, tile), tile)
        part = jnp.dot(
            ctx_all[...].reshape(n_exp * rows, ctx_ref.shape[1]), proj[:, cols],
            preferred_element_type=F32,
        ).reshape(n_exp, rows, tile)
        pown[:, :, cols] = part
        pbf[:, :, cols] = part.astype(BF16)
        return carry

    lax.fori_loop(0, proj.shape[1] // tile, project, 0)
    prs_c = [
        send(
            pbf.at[lax.rem(h + k, n_head)], prs.at[k - 1], prs_s.at[k], prs_r.at[k], on_head(k)
        )
        for k in range(1, n_head)
    ]
    for c in prs_c:
        c.start()
    for c in wz_c:
        c.wait()
    wt_c = send(wall.at[t], wall.at[t], wt_s, wt_r, on_tok)
    wt_c.start()

    @pl.when(jnp.logical_not(mine))
    def _():
        stream_c.wait()

    @pl.when(mine)
    def _():
        stream_t[...] = stream_bf[...]

    for c in prs_c:
        c.wait()
    attn = pown[h]
    for k in range(1, n_head):
        attn = attn + prs[k - 1].astype(F32)
    attn_buf[...] = attn
    attn_c = send(attn_buf, attn_in, at_s, at_r, turned)

    resid = attn + stream_t[...].astype(F32)
    gain = gain_ref[:, pl.ds(pl.multiple_of(e * width, LANES), width)]
    own_cols = pl.ds(pl.multiple_of(e * width, LANES), width)
    x[t, h, :, own_cols] = (resid * gain).astype(BF16)
    square = jnp.sum(resid * resid, axis=1, keepdims=True)
    row_id = lax.broadcasted_iota(jnp.int32, (rows, LANES), 0)
    flat = jnp.sum(jnp.where(row_id == lane, square, 0.0), axis=0, keepdims=True)
    ssq[t, h, e] = jnp.broadcast_to(flat, (8, LANES))

    def x_at(i, c):
        return x.at[t, i, :, pl.ds(pl.multiple_of(c * width, LANES), width)]

    xz_c = [
        send(x_at(h, e), x_at(h, e), xz_s.at[k], xz_r.at[k], on_exp(k)) for k in range(1, n_exp)
    ]
    qz_c = [
        send(ssq.at[t, h, e], ssq.at[t, h, e], qz_s.at[k], qz_r.at[k], on_exp(k))
        for k in range(1, n_exp)
    ]
    for a, b in zip(xz_c, qz_c):
        a.start()
        b.start()
    xh_c = []
    for j in range(n_exp):
        if j:
            xz_c[j - 1].wait_recv()
        piece = lax.rem(e - j + n_exp, n_exp)
        for k in range(1, n_head):
            c = send(x_at(h, piece), x_at(h, piece), xh_s.at[k, j], xh_r.at[k, j], on_head(k))
            c.start()
            xh_c.append((k, j, c))
    for c in qz_c:
        c.wait_recv()
    qh_c = [
        send(ssq.at[t, h], ssq.at[t, h], qh_s.at[k], qh_r.at[k], on_head(k))
        for k in range(1, n_head)
    ]
    for c in qh_c:
        c.start()

    @pl.when(jnp.logical_not(mine))
    def _():
        attn_c.start()

    xt_c = []
    for k in range(n_head):
        if k:
            for kk, j, c in xh_c:
                if kk == k:
                    c.wait_recv()
            qh_c[k - 1].wait_recv()
        image = lax.rem(h - k + n_head, n_head)
        a = send(x.at[t, image], x.at[t, image], xt_s.at[k], xt_r.at[k], on_tok)
        b = send(ssq.at[t, image], ssq.at[t, image], qt_s.at[k], qt_r.at[k], on_tok)
        a.start()
        b.start()
        xt_c += [a, b]
    for c in xt_c:
        c.wait_recv()
    wt_c.wait()

    total = jnp.sum(ssq[...], axis=2)[:, :, 0:1, :]
    wide = jnp.broadcast_to(
        total, (n_tok, n_exp, rows, LANES)
    ).reshape(tokens, LANES)
    token_row = lax.rem(lax.broadcasted_iota(jnp.int32, (tokens, LANES), 0), rows)
    token_lane = lax.broadcasted_iota(jnp.int32, (tokens, LANES), 1)
    sums = jnp.sum(jnp.where(token_row == token_lane, wide, 0.0), axis=1, keepdims=True)
    scale = lax.rsqrt(sums / model + eps_value)
    weights = wall[...].reshape(tokens, LANES)

    hid_tile = 256 if n_hid % 256 == 0 else n_hid
    col_tile = min(width, 512)
    per = width // col_tile

    def expert(j):
        for m in range(2):
            w_copy(3 * j + m).wait()
        gs, us, ds_ = (3 * j) % n_slots, (3 * j + 1) % n_slots, (3 * j + 2) % n_slots
        number = (t * n_exp + e) * n_local + j
        gate_w = jnp.sum(jnp.where(token_lane == number, weights, 0.0), axis=1, keepdims=True)

        def up(i, carry):
            span = pl.ds(pl.multiple_of(i * hid_tile, hid_tile), hid_tile)
            dims = (((1,), (1,)), ((), ()))
            xv = x[...].reshape(tokens, model)
            g = lax.dot_general(xv, wbuf[gs, span, :], dims, preferred_element_type=F32) * scale
            u = lax.dot_general(xv, wbuf[us, span, :], dims, preferred_element_type=F32) * scale
            value = g / (1.0 + jnp.exp(-g)) * u * gate_w
            hid[i] = value.astype(BF16)
            return carry

        lax.fori_loop(0, n_hid // hid_tile, up, 0)
        for m in range(2):
            if 3 * j + m + n_slots < 3 * n_local:
                w_copy(3 * j + m + n_slots).start()
        w_copy(3 * j + 2).wait()

        def down(cols):
            value = jnp.zeros((tokens, col_tile), F32)
            for i in range(n_hid // hid_tile):
                value = value + jnp.dot(
                    hid[i], wbuf[ds_, i * hid_tile : (i + 1) * hid_tile, cols],
                    preferred_element_type=F32,
                )
            value = value.reshape(n_tok, n_exp, rows, col_tile)
            if j:
                value = value + acc[:, :, :, cols]
            acc[:, :, :, cols] = value

        return down

    to_c = []
    for j in range(n_local):
        down = expert(j)
        if j < n_local - 1:

            def step(i, carry):
                down(pl.ds(pl.multiple_of(i * col_tile, col_tile), col_tile))
                return carry

            lax.fori_loop(0, model // col_tile, step, 0)
            if 3 * j + 2 + n_slots < 3 * n_local:
                w_copy(3 * j + 2 + n_slots).start()
            continue
        for k in range(n_head):
            chunk = lax.rem(h + 1 + k, n_head)

            def step(i, carry):
                down(pl.ds(pl.multiple_of(chunk * width + i * col_tile, col_tile), col_tile))
                return carry

            lax.fori_loop(0, per, step, 0)
            cols = pl.ds(pl.multiple_of(chunk * width, LANES), width)
            obf[k] = acc[tp, :, :, cols].astype(BF16)
            c = send(obf.at[k], tin.at[k], to_s.at[k], to_r.at[k], on_tok)
            c.start()
            to_c.append(c)

    ho_c = []
    for k in range(n_head):
        chunk = lax.rem(h + 1 + k, n_head)
        cols = pl.ds(pl.multiple_of(chunk * width, LANES), width)
        to_c[k].wait_recv()
        if k < n_head - 1:
            hsend[k] = (acc[t, :, :, cols] + tin[k].astype(F32)).astype(BF16)
            c = send(hsend.at[k], hrecv.at[k], ho_s.at[k], ho_r.at[k], on_head(k + 1))
            c.start()
            ho_c.append(c)
    for c in ho_c:
        c.wait_recv()

    own = pl.ds(pl.multiple_of(h * width, LANES), width)

    def mixed(image):
        value = acc[t, image, :, own] + tin[n_head - 1, image].astype(F32)
        for k in range(n_head - 1):
            value = value + hrecv[k, image].astype(F32)
        return value

    zo_c = []
    for k in range(1, n_exp):
        zsend[k - 1] = mixed(lax.rem(e + k, n_exp)).astype(BF16)
        c = send(zsend.at[k - 1], zrecv.at[k - 1], zo_s.at[k], zo_r.at[k], on_exp(k))
        c.start()
        zo_c.append(c)

    @pl.when(jnp.logical_not(mine))
    def _():
        attn_c.wait()

    @pl.when(mine)
    def _():
        attn_in[...] = attn_buf[...]

    value = mixed(e) + (stream_ref[...] + attn_in[...])
    for k in range(1, n_exp):
        zo_c[k - 1].wait_recv()
        value = value + zrecv[k - 1].astype(F32)
    out_ref[...] = value
    for c in xz_c + qz_c + [c for _, _, c in xh_c] + qh_c + xt_c + to_c + ho_c + zo_c:
        c.wait_send()


def solution(mesh):
    n_tok, n_head, n_exp = mesh.shape["tok"], mesh.shape["head"], mesh.shape["exp"]

    def on_device(
        context, out_proj, stream, norm_gain, expert_ids, slot_ids, gate_probs, w_gate, w_up, w_down
    ):
        rows, width = stream.shape[1:]
        n_local, n_hid, model = w_gate.shape
        n_slots = min(3 * n_local, SLOT_BYTES // (n_hid * model * 2))
        tokens = n_tok * n_exp * rows
        hid_tile = 256 if n_hid % 256 == 0 else n_hid
        vmem = pl.BlockSpec(memory_space=pltpu.VMEM)
        hbm = pl.BlockSpec(memory_space=pl.ANY)
        dma = pltpu.SemaphoreType.DMA
        V = pltpu.VMEM
        scratch = [
            V(out_proj.shape, BF16),
            V((n_slots, n_hid, model), BF16),
            V((n_exp, rows, context.shape[2]), BF16),
            V((n_tok, n_exp, rows, LANES), F32),
            V((rows, width), BF16),
            V((rows, width), BF16),
            V((n_exp, rows, width), BF16),
            V((n_exp, rows, width), F32),
            V((n_head - 1, rows, width), BF16),
            V((rows, width), F32),
            V((rows, width), F32),
            V((n_tok, n_exp, n_exp, 8, LANES), F32),
            V((n_tok, n_exp, rows, model), BF16),
            V((n_hid // hid_tile, tokens, hid_tile), BF16),
            V((n_tok, n_exp, rows, model), F32),
            V((n_head, n_exp, rows, width), BF16),
            V((n_head, n_exp, rows, width), BF16),
            V((n_head - 1, n_exp, rows, width), BF16),
            V((n_head - 1, n_exp, rows, width), BF16),
            V((n_exp - 1, rows, width), BF16),
            V((n_exp - 1, rows, width), BF16),
            dma, dma((n_slots,)),
            dma((n_exp,)), dma((n_exp,)), dma((n_exp,)), dma((n_exp,)), dma, dma, dma, dma,
            dma((n_head,)), dma((n_head,)), dma, dma,
            dma((n_exp,)), dma((n_exp,)), dma((n_exp,)), dma((n_exp,)),
            dma((n_head, n_exp)), dma((n_head, n_exp)), dma((n_head,)), dma((n_head,)),
            dma((n_head,)), dma((n_head,)), dma((n_head,)), dma((n_head,)),
            dma((n_head,)), dma((n_head,)), dma((n_head,)), dma((n_head,)),
            dma((n_exp,)), dma((n_exp,)),
        ]
        out = pl.pallas_call(
            functools.partial(kernel, n_tok, n_head, n_exp, n_slots),
            out_shape=jax.ShapeDtypeStruct((rows, width), F32),
            in_specs=[vmem, hbm, vmem, vmem, vmem, vmem, vmem, hbm, hbm, hbm],
            out_specs=vmem,
            scratch_shapes=scratch,
            compiler_params=pltpu.CompilerParams(
                collective_id=0, has_side_effects=True, vmem_limit_bytes=67_043_328
            ),
        )(
            context[0], out_proj, stream[0], norm_gain[None], expert_ids[0], slot_ids[0],
            gate_probs[0], w_gate, w_up, w_down,
        )
        return out[None]

    in_specs = (
        P("exp", "tok", "head"),
        P("head", "exp"),
        P("exp", "tok", "head"),
        P(),
        P("exp", "tok", None),
        P("exp", "tok", None),
        P("exp", "tok", None),
        P(("tok", "exp"), "head", None),
        P(("tok", "exp"), "head", None),
        P(("tok", "exp"), "head", None),
    )
    return jax.shard_map(
        on_device, mesh=mesh, in_specs=in_specs, out_specs=P("exp", "tok", "head"), check_vma=False
    )
```

time: 433 us -> 95.4 us (0.22)
  waiting for transfers between devices: 322 us -> 0 us
  Pallas kernels: 0 us -> 89.4 us
  matrix products: 45.4 us -> 0 us
  blocking collectives: 29.7 us -> 0 us
  between operations: 13.3 us -> 0.01 us
  starting transfers between devices: 5.89 us -> 0 us
  other arithmetic: 4.33 us -> 0 us
    all_gather x2 -> x0, waiting for transfers between devices: 201 us -> none  [the longest x1 149 us: on_device(): lax.all_gather(out_proj, 'exp', axis=1, tiled=True)]
    pallas_call x0 -> x1, Pallas kernels: none -> 89.4 us  [on_device(): pl.pallas_call(functools.partial(kernel, n_tok, n_head, n_exp, n_slots),...]
    reduce_scatter x1 -> x0, waiting for transfers between devices: 52.7 us -> none  [on_device(): lax.psum_scatter(widened.astype(jnp.bfloat16), 'head', scatter_dimension=...]
    dot_general x4 -> x0, matrix products: 45.4 us -> none  [the longest x1 13.6 us: on_device(): jnp.einsum('slch,lhd->slcd', hidden, w_down, preferred_element_type=jnp.f...]
    psum x1 -> x0, waiting for transfers between devices: 44.9 us -> none  [on_device(): resid_full = lax.psum(partial_value, 'head')]
    all_to_all x1 -> x0, blocking collectives: 29.7 us -> none  [on_device(): lax.all_to_all(outgoing, ('tok', 'exp'), split_axis=0, concat_axis=0, til...]
    all_to_all x1 -> x0, waiting for transfers between devices: 22.9 us -> none  [on_device(): lax.all_to_all(summed.reshape(EXPERTS, CAP, col_width).astype(jnp.bfloat1...]
    all_to_all x1 -> x0, starting transfers between devices: 5.59 us -> none  [on_device(): lax.all_to_all(summed.reshape(EXPERTS, CAP, col_width).astype(jnp.bfloat1...]
  transfers between devices with their start and end apart: 5 -> 0, of which waited for: 5 -> 0; matrix products, arithmetic and copies ran while one was open for 0% -> 0% of each run, Pallas kernels for 0% -> 0%
where the time goes in v1:
time: 95.4 us; the launch traced here: 95.1 us
  Pallas kernels  89.4 us (94%)
  local copies, waits for them, and re-layouts  5.65 us (6%)
    pallas_call x1, Pallas kernels, on_device(): pl.pallas_call(functools.partial(kernel, n_tok, n_head, n_exp, n_slots),...  89.4 us
    unnamed x4, local copies, waits for them, and re-layouts  5.65 us

profile of v1, /device:TPU:15, one launch (start us, length us, event | category | flops | bytes accessed | tf_op | source)
XLA Modules:
  0.0 95.1 jit_solution(18233146591261421075)
XLA Ops:
  0.0 1.4 %copy.11 = s32[1,32,8]{2,1,0:T(8,128)} copy(s32[1,32,8]{1,2,0:T(8,128)} %param.14) | data formatting | bytes 2048 | tf_op args[4]
  1.4 1.4 %copy.12 = s32[1,32,8]{2,1,0:T(8,128)} copy(s32[1,32,8]{1,2,0:T(8,128)} %param.15) | data formatting | bytes 2048 | tf_op args[5]
  2.7 1.4 %copy.13 = f32[1,32,8]{2,1,0:T(8,128)} copy(f32[1,32,8]{1,2,0:T(8,128)} %param.16) | data formatting | bytes 2048 | tf_op args[6]
  4.1 89.4 %shard_map.100 = f32[32,1024]{1,0:T(8,128)} custom-call(bf16[32,1024]{1,0:T(8,128)(2,1)} %bitcast.9, bf16[1024,1024]{1,0:T(8,128)(2,1)} %proj_hbm.1, f32[32,1024]{1,0:T(8,128)} %bitcast.8, f32[1,4096]{1,0:T(1,128)} %bitcast.13, s32[32,8]{1,0:T(8,128)} %bitcast.10, s32[32,8]{1,0:T(8,128)} %bitcast.11, f32[32,8]{1,0:T(8,128)} %bitcast.12, ...), custom_call_target="tpu_custom_call" | custom-call | tf_op jit(solution)/shard_map/pallas_call | solution.py:384
  93.5 1.6 %copy.15 = f32[1,32,1024]{2,1,0:T(8,128)} copy(f32[1,32,1024]{2,1,0:T(8,128)} %bitcast.7) | data formatting | bytes 262144

commit v2 on v1

--- a/solution.py
+++ b/solution.py
@@ -48,12 +48,11 @@
 
     on_tok = {"tok": tp}
 
-    sources = (wg_hbm, wu_hbm, wd_hbm)
+    sources = [s.at[j] for j in range(n_local) for s in (wg_hbm, wu_hbm)]
+    sources += [wd_hbm.at[j] for j in range(n_local)]
 
     def w_copy(q):
-        return pltpu.make_async_copy(
-            sources[q % 3].at[q // 3], wbuf.at[q % n_slots], w_sem.at[q % n_slots]
-        )
+        return pltpu.make_async_copy(sources[q], wbuf.at[q % n_slots], w_sem.at[q % n_slots])
 
     proj_copy = pltpu.make_async_copy(proj_hbm, proj, proj_sem)
     proj_copy.start()
@@ -69,15 +68,16 @@
     def _():
         pl.semaphore_signal(barrier, inc=1, device_id=turned, device_id_type=MESH)
 
-    for q in range(n_slots):
-        w_copy(q).start()
     stream_bf[...] = stream_ref[...].astype(BF16)
     lane = lax.broadcasted_iota(jnp.int32, (rows, LANES), 1)
-    dense = jnp.zeros((rows, LANES), F32)
-    for k in range(ids_ref.shape[1]):
-        hit = (ids_ref[:, k : k + 1] == lane) & (slots_ref[:, k : k + 1] >= 0)
-        dense = dense + jnp.where(hit, probs_ref[:, k : k + 1], 0.0)
-    wall[t, e] = dense
+    n_experts = wall.shape[2]
+    expert_row = lax.broadcasted_iota(jnp.int32, (n_experts, rows), 0)
+    dense = jnp.zeros((n_experts, rows), F32)
+    for k in range(ids_ref.shape[0]):
+        hit = (ids_ref[k : k + 1, :] == expert_row) & (slots_ref[k : k + 1, :] >= 0)
+        dense = dense + jnp.where(hit, probs_ref[k : k + 1, :], 0.0)
+    wall[0, e] = jnp.zeros((n_experts, LANES), F32)
+    wall[0, e, :, :rows] = dense
     ctx_all[e] = ctx_ref[...]
 
     @pl.when(mine)
@@ -100,7 +100,7 @@
         stream_c.start()
 
     wz_c = [
-        send(wall.at[t, e], wall.at[t, e], wz_s.at[k], wz_r.at[k], on_exp(k))
+        send(wall.at[0, e], wall.at[0, e], wz_s.at[k], wz_r.at[k], on_exp(k))
         for k in range(1, n_exp)
     ]
     for c in wz_c:
@@ -130,9 +130,11 @@
     ]
     for c in prs_c:
         c.start()
+    for q in range(n_slots):
+        w_copy(q).start()
     for c in wz_c:
         c.wait()
-    wt_c = send(wall.at[t], wall.at[t], wt_s, wt_r, on_tok)
+    wt_c = send(wall.at[0], wall.at[1], wt_s, wt_r, on_tok)
     wt_c.start()
 
     @pl.when(jnp.logical_not(mine))
@@ -154,20 +156,20 @@
     resid = attn + stream_t[...].astype(F32)
     gain = gain_ref[:, pl.ds(pl.multiple_of(e * width, LANES), width)]
     own_cols = pl.ds(pl.multiple_of(e * width, LANES), width)
-    x[t, h, :, own_cols] = (resid * gain).astype(BF16)
+    x[0, h, :, own_cols] = (resid * gain).astype(BF16)
     square = jnp.sum(resid * resid, axis=1, keepdims=True)
     row_id = lax.broadcasted_iota(jnp.int32, (rows, LANES), 0)
     flat = jnp.sum(jnp.where(row_id == lane, square, 0.0), axis=0, keepdims=True)
-    ssq[t, h, e] = jnp.broadcast_to(flat, (8, LANES))
+    ssq[0, h, e] = jnp.broadcast_to(flat, (8, LANES))
 
     def x_at(i, c):
-        return x.at[t, i, :, pl.ds(pl.multiple_of(c * width, LANES), width)]
+        return x.at[0, i, :, pl.ds(pl.multiple_of(c * width, LANES), width)]
 
     xz_c = [
         send(x_at(h, e), x_at(h, e), xz_s.at[k], xz_r.at[k], on_exp(k)) for k in range(1, n_exp)
     ]
     qz_c = [
-        send(ssq.at[t, h, e], ssq.at[t, h, e], qz_s.at[k], qz_r.at[k], on_exp(k))
+        send(ssq.at[0, h, e], ssq.at[0, h, e], qz_s.at[k], qz_r.at[k], on_exp(k))
         for k in range(1, n_exp)
     ]
     for a, b in zip(xz_c, qz_c):
@@ -185,7 +187,7 @@
     for c in qz_c:
         c.wait_recv()
     qh_c = [
-        send(ssq.at[t, h], ssq.at[t, h], qh_s.at[k], qh_r.at[k], on_head(k))
+        send(ssq.at[0, h], ssq.at[0, h], qh_s.at[k], qh_r.at[k], on_head(k))
         for k in range(1, n_head)
     ]
     for c in qh_c:
@@ -203,8 +205,8 @@
                     c.wait_recv()
             qh_c[k - 1].wait_recv()
         image = lax.rem(h - k + n_head, n_head)
-        a = send(x.at[t, image], x.at[t, image], xt_s.at[k], xt_r.at[k], on_tok)
-        b = send(ssq.at[t, image], ssq.at[t, image], qt_s.at[k], qt_r.at[k], on_tok)
+        a = send(x.at[0, image], x.at[1, image], xt_s.at[k], xt_r.at[k], on_tok)
+        b = send(ssq.at[0, image], ssq.at[1, image], qt_s.at[k], qt_r.at[k], on_tok)
         a.start()
         b.start()
         xt_c += [a, b]
@@ -212,26 +214,29 @@
         c.wait_recv()
     wt_c.wait()
 
-    total = jnp.sum(ssq[...], axis=2)[:, :, 0:1, :]
-    wide = jnp.broadcast_to(
-        total, (n_tok, n_exp, rows, LANES)
-    ).reshape(tokens, LANES)
     token_row = lax.rem(lax.broadcasted_iota(jnp.int32, (tokens, LANES), 0), rows)
     token_lane = lax.broadcasted_iota(jnp.int32, (tokens, LANES), 1)
-    sums = jnp.sum(jnp.where(token_row == token_lane, wide, 0.0), axis=1, keepdims=True)
+
+    def column(value):
+        wide = jnp.broadcast_to(value, (n_tok, n_exp, rows, LANES)).reshape(tokens, LANES)
+        return jnp.sum(jnp.where(token_row == token_lane, wide, 0.0), axis=1, keepdims=True)
+
+    sums = column(jnp.sum(ssq[...], axis=2)[:, :, 0:1, :])
     scale = lax.rsqrt(sums / model + eps_value)
-    weights = wall[...].reshape(tokens, LANES)
+    expert_of = lax.broadcasted_iota(jnp.int32, wall.shape, 2)
 
     hid_tile = 256 if n_hid % 256 == 0 else n_hid
     col_tile = min(width, 512)
     per = width // col_tile
 
-    def expert(j):
+    n_tiles = n_hid // hid_tile
+    for j in range(n_local):
         for m in range(2):
-            w_copy(3 * j + m).wait()
-        gs, us, ds_ = (3 * j) % n_slots, (3 * j + 1) % n_slots, (3 * j + 2) % n_slots
+            w_copy(2 * j + m).wait()
+        gs, us = (2 * j) % n_slots, (2 * j + 1) % n_slots
         number = (t * n_exp + e) * n_local + j
-        gate_w = jnp.sum(jnp.where(token_lane == number, weights, 0.0), axis=1, keepdims=True)
+        picked = jnp.where(expert_of == number, wall[...], 0.0)
+        gate_w = column(jnp.sum(picked, axis=2, keepdims=True))
 
         def up(i, carry):
             span = pl.ds(pl.multiple_of(i * hid_tile, hid_tile), hid_tile)
@@ -240,73 +245,62 @@
             g = lax.dot_general(xv, wbuf[gs, span, :], dims, preferred_element_type=F32) * scale
             u = lax.dot_general(xv, wbuf[us, span, :], dims, preferred_element_type=F32) * scale
             value = g / (1.0 + jnp.exp(-g)) * u * gate_w
-            hid[i] = value.astype(BF16)
+            hid[j * n_tiles + i] = value.astype(BF16)
             return carry
 
-        lax.fori_loop(0, n_hid // hid_tile, up, 0)
+        lax.fori_loop(0, n_tiles, up, 0)
         for m in range(2):
-            if 3 * j + m + n_slots < 3 * n_local:
-                w_copy(3 * j + m + n_slots).start()
-        w_copy(3 * j + 2).wait()
-
-        def down(cols):
-            value = jnp.zeros((tokens, col_tile), F32)
-            for i in range(n_hid // hid_tile):
-                value = value + jnp.dot(
-                    hid[i], wbuf[ds_, i * hid_tile : (i + 1) * hid_tile, cols],
-                    preferred_element_type=F32,
-                )
-            value = value.reshape(n_tok, n_exp, rows, col_tile)
-            if j:
-                value = value + acc[:, :, :, cols]
-            acc[:, :, :, cols] = value
-
-        return down
-
+            if 2 * j + m + n_slots < 3 * n_local:
+                w_copy(2 * j + m + n_slots).start()
+
+    for j in range(n_local):
+        w_copy(2 * n_local + j).wait()
+    ho_c = []
     to_c = []
-    for j in range(n_local):
-        down = expert(j)
-        if j < n_local - 1:
-
-            def step(i, carry):
-                down(pl.ds(pl.multiple_of(i * col_tile, col_tile), col_tile))
-                return carry
-
-            lax.fori_loop(0, model // col_tile, step, 0)
-            if 3 * j + 2 + n_slots < 3 * n_local:
-                w_copy(3 * j + 2 + n_slots).start()
-            continue
-        for k in range(n_head):
-            chunk = lax.rem(h + 1 + k, n_head)
-
-            def step(i, carry):
-                down(pl.ds(pl.multiple_of(chunk * width + i * col_tile, col_tile), col_tile))
-                return carry
-
-            lax.fori_loop(0, per, step, 0)
-            cols = pl.ds(pl.multiple_of(chunk * width, LANES), width)
-            obf[k] = acc[tp, :, :, cols].astype(BF16)
-            c = send(obf.at[k], tin.at[k], to_s.at[k], to_r.at[k], on_tok)
-            c.start()
-            to_c.append(c)
-
-    ho_c = []
-    for k in range(n_head):
-        chunk = lax.rem(h + 1 + k, n_head)
-        cols = pl.ds(pl.multiple_of(chunk * width, LANES), width)
+
+    def head_step(k):
         to_c[k].wait_recv()
         if k < n_head - 1:
-            hsend[k] = (acc[t, :, :, cols] + tin[k].astype(F32)).astype(BF16)
+            hsend[k] = (acc[k] + tin[k].astype(F32)).astype(BF16)
             c = send(hsend.at[k], hrecv.at[k], ho_s.at[k], ho_r.at[k], on_head(k + 1))
             c.start()
             ho_c.append(c)
+
+    for k in range(n_head):
+        chunk = lax.rem(h + 1 + k, n_head)
+
+        def step(i, carry):
+            part = pl.ds(pl.multiple_of(i * col_tile, col_tile), col_tile)
+            cols = pl.ds(pl.multiple_of(chunk * width + i * col_tile, col_tile), col_tile)
+            value = jnp.zeros((tokens, col_tile), F32)
+            for j in range(n_local):
+                for i in range(n_tiles):
+                    value = value + jnp.dot(
+                        hid[j * n_tiles + i],
+                        wbuf[
+                            (2 * n_local + j) % n_slots, i * hid_tile : (i + 1) * hid_tile, cols
+                        ],
+                        preferred_element_type=F32,
+                    )
+            value = value.reshape(n_tok, n_exp, rows, col_tile)
+            acc[k, :, :, part] = value[0]
+            obf[k, :, :, part] = value[1].astype(BF16)
+            return carry
+
+        lax.fori_loop(0, per, step, 0)
+        c = send(obf.at[k], tin.at[k], to_s.at[k], to_r.at[k], on_tok)
+        c.start()
+        to_c.append(c)
+        if k:
+            head_step(k - 1)
+    head_step(n_head - 1)
+
     for c in ho_c:
         c.wait_recv()
 
-    own = pl.ds(pl.multiple_of(h * width, LANES), width)
 
     def mixed(image):
-        value = acc[t, image, :, own] + tin[n_head - 1, image].astype(F32)
+        value = acc[n_head - 1, image] + tin[n_head - 1, image].astype(F32)
         for k in range(n_head - 1):
             value = value + hrecv[k, image].astype(F32)
         return value
@@ -326,7 +320,7 @@
     def _():
         attn_in[...] = attn_buf[...]
 
-    value = mixed(e) + (stream_ref[...] + attn_in[...])
+    value = mixed(e) + attn_in[...]
     for k in range(1, n_exp):
         zo_c[k - 1].wait_recv()
         value = value + zrecv[k - 1].astype(F32)
@@ -354,7 +348,7 @@
             V(out_proj.shape, BF16),
             V((n_slots, n_hid, model), BF16),
             V((n_exp, rows, context.shape[2]), BF16),
-            V((n_tok, n_exp, rows, LANES), F32),
+            V((n_tok, n_exp, n_tok * n_exp * n_local, LANES), F32),
             V((rows, width), BF16),
             V((rows, width), BF16),
             V((n_exp, rows, width), BF16),
@@ -364,8 +358,8 @@
             V((rows, width), F32),
             V((n_tok, n_exp, n_exp, 8, LANES), F32),
             V((n_tok, n_exp, rows, model), BF16),
-            V((n_hid // hid_tile, tokens, hid_tile), BF16),
-            V((n_tok, n_exp, rows, model), F32),
+            V((n_local * (n_hid // hid_tile), tokens, hid_tile), BF16),
+            V((n_head, n_exp, rows, width), F32),
             V((n_head, n_exp, rows, width), BF16),
             V((n_head, n_exp, rows, width), BF16),
             V((n_head - 1, n_exp, rows, width), BF16),
@@ -391,10 +385,10 @@
                 collective_id=0, has_side_effects=True, vmem_limit_bytes=67_043_328
             ),
         )(
-            context[0], out_proj, stream[0], norm_gain[None], expert_ids[0], slot_ids[0],
-            gate_probs[0], w_gate, w_up, w_down,
+            context[0], out_proj, stream[0], norm_gain[None], expert_ids[0].T, slot_ids[0].T,
+            gate_probs[0].T, w_gate, w_up, w_down,
         )
-        return out[None]
+        return stream + out[None]
 
     in_specs = (
         P("exp", "tok", "head"),

time: 95.4 us -> 83.5 us (0.88)
  Pallas kernels: 89.4 us -> 81.7 us
  local copies, waits for them, and re-layouts: 5.65 us -> 0 us
  other arithmetic: 0 us -> 1.64 us
    pallas_call x1, Pallas kernels: 89.4 us -> 81.7 us  [on_device(): pl.pallas_call(functools.partial(kernel, n_tok, n_head, n_exp, n_slots),...]
    unnamed x4 -> x0, local copies, waits for them, and re-layouts: 5.65 us -> none
    add x0 -> x1, other arithmetic: none -> 1.64 us  [on_device(): return stream + out[None]]
where the time goes in v2:
time: 83.5 us; the launch traced here: 83.4 us
  Pallas kernels  81.7 us (98%)
  other arithmetic  1.64 us (2%)
    pallas_call x1, Pallas kernels, on_device(): pl.pallas_call(functools.partial(kernel, n_tok, n_head, n_exp, n_slots),...  81.7 us

profile of v2, /device:TPU:15, one launch (start us, length us, event | category | flops | bytes accessed | tf_op | source)
XLA Modules:
  0.0 83.4 jit_solution(6721130567905439664)
XLA Ops:
  0.0 81.7 %shard_map.100 = f32[32,1024]{1,0:T(8,128)} custom-call(bf16[32,1024]{1,0:T(8,128)(2,1)} %bitcast.15, bf16[1024,1024]{1,0:T(8,128)(2,1)} %proj_hbm.1, f32[32,1024]{1,0:T(8,128)} %bitcast.14, f32[1,4096]{1,0:T(1,128)} %bitcast.16, s32[8,32]{1,0:T(8,128)} %bitcast.17, s32[8,32]{1,0:T(8,128)} %bitcast.18, f32[8,32]{1,0:T(8,128)} %bitcast.19, ...), custom_call_target="tpu_custom_call" | custom-call | tf_op jit(solution)/shard_map/pallas_call | solution.py:378
  81.7 1.6 %bitcast_add_fusion = f32[1,32,1024]{2,1,0:T(8,128)} fusion(f32[1,32,1024]{2,1,0:T(8,128)} %param.12, f32[32,1024]{1,0:T(8,128)} %shard_map.100), kind=kLoop, calls=%fused_computation | loop fusion | flops 32768 | bytes 393216 | tf_op jit(solution)/shard_map/add | solution.py:391
